TPU v7x, 512 devices: a whole 4x4x16 slice. The times are simulated.
512 devices in a mesh: stream: 32 (over z, core), xsec: 16 (over y, x).
Axes of the slice: x: 4, y: 4, z: 16, core: 2. Of those that a mesh axis runs over, the one named last changes fastest.
Arguments:
- right_sides: float32 [32, 2048, 2048], P('stream', None, 'xsec'), may hold values from -6 to 6
- lower_first: bfloat16 [32, 2048, 2048], P('stream', None, 'xsec'), may hold values from -0.0625 to 0.0625
- upper_first: bfloat16 [32, 2048, 2048], P('stream', None, 'xsec'), may hold values from -0.0625 to 0.0625
- lower_second: bfloat16 [32, 2048, 2048], P('stream', None, 'xsec'), may hold values from -0.0625 to 0.0625
- upper_second: bfloat16 [32, 2048, 2048], P('stream', None, 'xsec'), may hold values from -0.0625 to 0.0625
Outputs:
- reduced: float32 [32, 2048, 2048], P('stream', None, 'xsec')
All inputs are finite; a program needn't handle non-finite values.
Results may differ from a plain program's by a relative error of at most 0.0023.
Values may be sent and summed in bfloat16 or wider, within the bound.
No kernel may reach another device: no remote copies, remote signals or barrier semaphores. Data moves between devices by JAX's collectives and lax.ppermute only.
A program may use at most 128 MiB of HBM per device.

v0:
```python
import jax
import jax.numpy as jnp
from jax import lax
from jax.sharding import PartitionSpec as P


def extended(value, sides, width):
    for axis, dim in sides:
        size, length = (lax.axis_size(axis), value.shape[dim])
        up = [(i, (i + 1) % size) for i in range(size - 1)]
        down = [(j, i) for i, j in up]
        last = lax.slice_in_dim(value, length - width, length, axis=dim)
        first = lax.slice_in_dim(value, 0, width, axis=dim)
        before = lax.ppermute(last, axis, up)
        after = lax.ppermute(first, axis, down)
        value = jnp.concatenate([before, value, after], axis=dim)
    return value


def shifted(value, axis, steps):
    count = lax.axis_size(axis)
    first, last = (max(0, -steps), min(count, count - steps))
    return lax.ppermute(value, axis, [(source, source + steps) for source in range(first, last)])


def neighbours_near(outgoing):
    padded = extended(outgoing[None], (("stream", 0),), 1)
    return (padded[0], padded[2])


def neighbours_far(outgoing):
    from_below = shifted(outgoing, "stream", 2)
    from_above = shifted(outgoing, "stream", -2)
    return (from_below, from_above)


def reduce_level(current, lower_blocks, upper_blocks, neighbours):
    outgoing = current.astype(jnp.bfloat16)
    from_below, from_above = neighbours(outgoing)
    lower_piece = lax.all_gather(lower_blocks, "xsec", axis=2, tiled=True)
    upper_piece = lax.all_gather(upper_blocks, "xsec", axis=2, tiled=True)
    total = jnp.dot(lower_piece[0], from_below, preferred_element_type=jnp.float32)
    total = total + jnp.dot(upper_piece[0], from_above, preferred_element_type=jnp.float32)
    return current + total


def on_device(right_sides, lower_first, upper_first, lower_second, upper_second):
    level_one = reduce_level(right_sides[0], lower_first, upper_first, neighbours_near)
    level_two = reduce_level(level_one, lower_second, upper_second, neighbours_far)
    return level_two[None]


def solution(mesh):
    return jax.shard_map(
        on_device,
        mesh=mesh,
        in_specs=(
            P("stream", None, "xsec"),
            P("stream", None, "xsec"),
            P("stream", None, "xsec"),
            P("stream", None, "xsec"),
            P("stream", None, "xsec"),
        ),
        out_specs=P("stream", None, "xsec"),
        check_vma=False,
    )
```

profile of v0, /device:TPU:1, one launch (start us, length us, event | category | flops | bytes accessed | tf_op | source)
XLA Modules:
  0.0 410.1 jit_solution(17927725365922115572)
XLA Ops:
  6.5 0.0 copy-start
  6.5 0.0 all-gather.7.cloned.1.call-start
  6.5 0.7 all-gather.7.cloned.1.call-update
  7.3 0.0 all-gather.5.cloned.1.call-start
  7.3 0.7 all-gather.5.cloned.1.call-update
  8.0 0.0 all-gather.11.cloned.1.call-start
  8.1 0.7 all-gather.11.cloned.1.call-update
  8.7 0.0 all-gather.9.cloned.1.call-start
  8.8 0.5 all-gather.9.cloned.1.call-update
  9.3 1.3 convert_element_type.7
  10.6 8.8 %collective-permute-start.1 = (bf16[1,2048,128]{2,1,0:T(8,128)(2,1)S(1)}, bf16[1,2048,128]{2,1,0:T(8,128)(2,1)}, u32[]{:S(2)}, u32[]{:S(2)}) collective-permute-start(bf16[1,2048,128]{2,1,0:T(8,128)(2,1)S(1)} %convert_element_type.7), channel_id=1, source_target_pairs={{16,0},{32,16},{48,32},{64,48},{80,64},{96,80},{112,96},{128,112},... | collective-permute-start | bytes 1572872 | tf_op jit(solution)/shard_map/ppermute | solution.py:15
  19.4 1.9 collective-permute-start
  21.3 1.2 collective-permute-done.1
  22.5 86.0 %all-gather.7.cloned.1.call-done = bf16[1,2048,2048]{2,1,0:T(8,128)(2,1)} async-done(((bf16[1,2048,128]{2,1,0:T(8,128)(2,1)}), bf16[1,2048,2048]{2,1,0:T(8,128)(2,1)}) %all-gather.7.cloned.1.call-update) | async-done | bytes 8388624 | tf_op jit(solution)/shard_map/all_gather | solution.py:41
  108.5 5.8 %fusion.4 = f32[2048,128]{1,0:T(8,128)S(1)} fusion(bf16[1,2048,2048]{2,1,0:T(8,128)(2,1)} %all-gather.7.cloned.1.call-done, bf16[1,2048,128]{2,1,0:T(8,128)(2,1)} %collective-permute-done.1), kind=kOutput, calls=%fused_computation.4 | convolution fusion | flops 1073741824 | bytes 9961472 | tf_op jit(solution)/shard_map/dot_general | solution.py:43
  114.2 0.0 collective-permute-done
  114.3 0.0 copy-start.1
  114.3 0.8 copy-done.1
  115.1 89.6 %all-gather.5.cloned.1.call-done = bf16[1,2048,2048]{2,1,0:T(8,128)(2,1)} async-done(((bf16[1,2048,128]{2,1,0:T(8,128)(2,1)}), bf16[1,2048,2048]{2,1,0:T(8,128)(2,1)}) %all-gather.5.cloned.1.call-update) | async-done | bytes 8388624 | tf_op jit(solution)/shard_map/all_gather | solution.py:40
  204.6 0.0 copy-done
  204.6 6.6 %fusion.28 = (bf16[2048,128]{1,0:T(8,128)(2,1)}, f32[2048,128]{1,0:T(8,128)S(1)}) fusion(f32[2048,128]{1,0:T(8,128)S(1)} %fusion.4, bf16[1,2048,128]{2,1,0:T(8,128)(2,1)} %copy-done.1, bf16[1,2048,2048]{2,1,0:T(8,128)(2,1)} %all-gather.5.cloned.1.call-done, f32[1,2048,128]{2,1,0:T(8,128)S(1)} %copy-done), kind=kOutput, calls=%fused_computation.16 | convolution fusion | flops 1074528256 | bytes 12582912 | tf_op jit(solution)/shard_map/dot_general | solution.py:42
  211.3 1.3 collective-permute-start.3
  212.6 4.0 collective-permute-start.2
  216.6 84.2 %all-gather.11.cloned.1.call-done = bf16[1,2048,2048]{2,1,0:T(8,128)(2,1)} async-done(((bf16[1,2048,128]{2,1,0:T(8,128)(2,1)}), bf16[1,2048,2048]{2,1,0:T(8,128)(2,1)}) %all-gather.11.cloned.1.call-update) | async-done | bytes 8388624 | tf_op jit(solution)/shard_map/all_gather | solution.py:41
  300.8 0.0 collective-permute-done.3
  300.8 5.7 %fusion = f32[128,2048]{0,1:T(8,128)S(1)} fusion(bf16[2048,128]{1,0:T(8,128)(2,1)S(1)} %collective-permute-done.3, bf16[1,2048,2048]{2,1,0:T(8,128)(2,1)} %all-gather.11.cloned.1.call-done), kind=kOutput, calls=%fused_computation | convolution fusion | flops 1073741824 | bytes 9961472 | tf_op jit(solution)/shard_map/dot_general | solution.py:43
  306.6 90.3 %all-gather.9.cloned.1.call-done = bf16[1,2048,2048]{2,1,0:T(8,128)(2,1)} async-done(((bf16[1,2048,128]{2,1,0:T(8,128)(2,1)}), bf16[1,2048,2048]{2,1,0:T(8,128)(2,1)}) %all-gather.9.cloned.1.call-update) | async-done | bytes 8388624 | tf_op jit(solution)/shard_map/all_gather | solution.py:40
  396.9 0.0 collective-permute-done.2
  396.9 6.7 %fusion.20 = f32[1,2048,128]{2,1,0:T(8,128)} fusion(f32[2048,128]{1,0:T(8,128)S(1)} %get-tuple-element.6, f32[128,2048]{0,1:T(8,128)S(1)} %fusion, bf16[2048,128]{1,0:T(8,128)(2,1)S(1)} %collective-permute-done.2, bf16[1,2048,2048]{2,1,0:T(8,128)(2,1)} %all-gather.9.cloned.1.call-done), kind=kOutput, calls=%fused_computation.12 | convolution fusion | flops 1074266112 | bytes 12058624 | tf_op jit(solution)/shard_map/dot_general | solution.py:42
Async XLA Ops:
  6.5 198.1 %copy-start = (f32[1,2048,128]{2,1,0:T(8,128)S(1)}, f32[1,2048,128]{2,1,0:T(8,128)}, u32[]{:S(2)}) copy-start(f32[1,2048,128]{2,1,0:T(8,128)} %param.5) | copy-start | bytes 3145732
  6.5 101.9 %all-gather.7.cloned.1.call-start = ((), (), s32[]{:S(2)}) async-start(), calls=%async_computation.1 | async-start | bytes 8912896 | tf_op jit(solution)/shard_map/all_gather | solution.py:41
  7.3 197.4 %all-gather.5.cloned.1.call-start = ((), (), s32[]{:S(2)}) async-start(), calls=%async_computation | async-start | bytes 8912896 | tf_op jit(solution)/shard_map/all_gather | solution.py:40
  8.0 292.8 %all-gather.11.cloned.1.call-start = ((), (), s32[]{:S(2)}) async-start(), calls=%async_computation.3 | async-start | bytes 8912896 | tf_op jit(solution)/shard_map/all_gather | solution.py:41
  8.7 388.1 %all-gather.9.cloned.1.call-start = ((), (), s32[]{:S(2)}) async-start(), calls=%async_computation.2 | async-start | bytes 8912896 | tf_op jit(solution)/shard_map/all_gather | solution.py:40
  10.6 11.9 %collective-permute-start.1 = (bf16[1,2048,128]{2,1,0:T(8,128)(2,1)S(1)}, bf16[1,2048,128]{2,1,0:T(8,128)(2,1)}, u32[]{:S(2)}, u32[]{:S(2)}) collective-permute-start(bf16[1,2048,128]{2,1,0:T(8,128)(2,1)S(1)} %convert_element_type.7), channel_id=1, source_target_pairs={{16,0},{32,16},{48,32},{64,48},{80,64},{96,80},{112,96},{128,112},... | collective-permute-start | bytes 1572872 | tf_op jit(solution)/shard_map/ppermute | solution.py:15
  19.4 94.9 %collective-permute-start = (bf16[1,2048,128]{2,1,0:T(8,128)(2,1)S(1)}, bf16[1,2048,128]{2,1,0:T(8,128)(2,1)S(1)}, u32[]{:S(2)}, u32[]{:S(2)}) collective-permute-start(bf16[1,2048,128]{2,1,0:T(8,128)(2,1)S(1)} %convert_element_type.7), channel_id=1, source_target_pairs={{0,16},{16,32},{32,48},{48,64},{64,80},{80,96},{96,112},{112,128},... | collective-permute-start | bytes 1572872 | tf_op jit(solution)/shard_map/ppermute | solution.py:14
  114.3 0.8 copy-start.1
  211.3 89.6 %collective-permute-start.3 = (bf16[2048,128]{1,0:T(8,128)(2,1)}, bf16[2048,128]{1,0:T(8,128)(2,1)S(1)}, u32[]{:S(2)}, u32[]{:S(2)}) collective-permute-start(bf16[2048,128]{1,0:T(8,128)(2,1)} %get-tuple-element.5), channel_id=1, source_target_pairs={{32,0},{48,16},{64,32},{80,48},{96,64},{112,80},{128,96},{144,112}... | collective-permute-start | bytes 1572872 | tf_op jit(solution)/shard_map/ppermute | solution.py:23
  212.6 184.3 %collective-permute-start.2 = (bf16[2048,128]{1,0:T(8,128)(2,1)}, bf16[2048,128]{1,0:T(8,128)(2,1)S(1)}, u32[]{:S(2)}, u32[]{:S(2)}) collective-permute-start(bf16[2048,128]{1,0:T(8,128)(2,1)} %get-tuple-element.5), channel_id=1, source_target_pairs={{0,32},{16,48},{32,64},{48,80},{64,96},{80,112},{96,128},{112,144}... | collective-permute-start | bytes 1572872 | tf_op jit(solution)/shard_map/ppermute | solution.py:23
Sparse Core Ops, SparseCore 0:
  10.3 98.0 all-gather.6
  111.5 93.1 all-gather.4
  207.6 93.1 all-gather.10
  303.7 93.1 all-gather.8
where the time goes:
time: 410 us
  waiting for transfers between devices  354 us (86%)
  matrix products  24.8 us (6%)
  starting transfers between devices  16.1 us (4%)
  between operations  13.2 us (3%)
    all_gather x2, waiting for transfers between devices, reduce_level(): lower_piece = lax.all_gather(lower_blocks, 'xsec', axis=2, tiled=True)  180 us
    all_gather x2, waiting for transfers between devices, reduce_level(): upper_piece = lax.all_gather(upper_blocks, 'xsec', axis=2, tiled=True)  170 us
    dot_general x2, matrix products, reduce_level(): jnp.dot(lower_piece[0], from_below, preferred_element_type=jnp.float32)  13.3 us
    dot_general x2, matrix products, reduce_level(): jnp.dot(upper_piece[0], from_above, preferred_element_type=jnp.float32)  11.5 us
    ppermute x1, starting transfers between devices, extended(): after = lax.ppermute(first, axis, down)  8.79 us
  transfers between devices with their start and end apart: 8, of which 5 were waited for; matrix products, arithmetic and copies ran while one was open for 5% of the time, Pallas kernels for 0%

commit v1 on v0

--- a/solution.py
+++ b/solution.py
@@ -38,7 +38,30 @@
     outgoing = current.astype(jnp.bfloat16)
     from_below, from_above = neighbours(outgoing)
     lower_piece = lax.all_gather(lower_blocks, "xsec", axis=2, tiled=True)
-    upper_piece = lax.all_gather(upper_blocks, "xsec", axis=2, tiled=True)
+    size_2, position, extent = (
+        lax.axis_size("xsec"),
+        lax.axis_index("xsec"),
+        upper_blocks.shape[2],
+    )
+    right = [(i_2, (i_2 + 1) % size_2) for i_2 in range(size_2)]
+    behind = [(i_2, (i_2 - 1) % size_2) for i_2 in range(size_2)]
+    out = jnp.zeros(
+        (*upper_blocks.shape[:2], size_2 * extent, *upper_blocks.shape[2 + 1 :]), upper_blocks.dtype
+    )
+    out = lax.dynamic_update_slice_in_dim(out, upper_blocks, position * extent, axis=2)
+    from_left = from_right = upper_blocks
+    half = size_2 // 2
+    for step in range(1, half + 1):
+        from_left = lax.ppermute(from_left, "xsec", right)
+        out = lax.dynamic_update_slice_in_dim(
+            out, from_left, (position - step) % size_2 * extent, axis=2
+        )
+        if step < size_2 - half:
+            from_right = lax.ppermute(from_right, "xsec", behind)
+            out = lax.dynamic_update_slice_in_dim(
+                out, from_right, (position + step) % size_2 * extent, axis=2
+            )
+    upper_piece = out
     total = jnp.dot(lower_piece[0], from_below, preferred_element_type=jnp.float32)
     total = total + jnp.dot(upper_piece[0], from_above, preferred_element_type=jnp.float32)
     return current + total

time: 410 us -> 368 us (0.90)
  waiting for transfers between devices: 354 us -> 176 us
  starting transfers between devices: 16.1 us -> 107 us
  local copies, waits for them, and re-layouts: 0.79 us -> 43.7 us
    all_gather x2 -> x0, waiting for transfers between devices: 170 us -> none  [reduce_level(): upper_piece = lax.all_gather(upper_blocks, 'xsec', axis=2, tiled=True)]
    ppermute x0 -> x30, starting transfers between devices: none -> 90.8 us  [the longest x14 57.6 us: reduce_level(): from_right = lax.ppermute(from_right, 'xsec', behind)]
    all_gather x2, waiting for transfers between devices: 180 us -> 118 us  [reduce_level(): lower_piece = lax.all_gather(lower_blocks, 'xsec', axis=2, tiled=True)]
    ppermute x0 -> x30, waiting for transfers between devices: none -> 52.9 us  [the longest x16 51.8 us: reduce_level(): from_left = lax.ppermute(from_left, 'xsec', right)]
    dynamic_update_slice x0 -> x32, local copies, waits for them, and re-layouts: none -> 34.2 us  [the longest x16 17.6 us: reduce_level(): lax.dynamic_update_slice_in_dim(out, from_left, (position - step) % size_...]
    squeeze x0 -> x2, local copies, waits for them, and re-layouts: none -> 8.65 us  [reduce_level(): upper_piece[0]]
    ppermute x2, waiting for transfers between devices: 0.01 us -> 4.56 us  [shifted(): lax.ppermute(value, axis, [(source, source + steps) for source in range(f...]
  transfers between devices with their start and end apart: 8 -> 36, of which waited for: 5 -> 18; matrix products, arithmetic and copies ran while one was open for 5% -> 17% of each run, Pallas kernels for 0% -> 0%
where the time goes in v1:
time: 368 us; the launch traced here: 367 us
  waiting for transfers between devices  176 us (48%)
  starting transfers between devices  107 us (29%)
  local copies, waits for them, and re-layouts  43.7 us (12%)
  matrix products  25.3 us (7%)
  between operations  13.8 us (4%)
    all_gather x2, waiting for transfers between devices, reduce_level(): lower_piece = lax.all_gather(lower_blocks, 'xsec', axis=2, tiled=True)  118 us
    ppermute x14, starting transfers between devices, reduce_level(): from_right = lax.ppermute(from_right, 'xsec', behind)  57.6 us
    ppermute x16, waiting for transfers between devices, reduce_level(): from_left = lax.ppermute(from_left, 'xsec', right)  51.8 us
    ppermute x16, starting transfers between devices, reduce_level(): from_left = lax.ppermute(from_left, 'xsec', right)  33.2 us
    dynamic_update_slice x16, local copies, waits for them, and re-layouts, reduce_level(): lax.dynamic_update_slice_in_dim(out, from_left, (position - step) % size_...  17.6 us
    dynamic_update_slice x14, local copies, waits for them, and re-layouts, reduce_level(): lax.dynamic_update_slice_in_dim(out, from_right, (position + step) % size...  14.8 us
    dot_general x2, matrix products, reduce_level(): jnp.dot(lower_piece[0], from_below, preferred_element_type=jnp.float32)  13.3 us
    dot_general x2, matrix products, reduce_level(): jnp.dot(upper_piece[0], from_above, preferred_element_type=jnp.float32)  12 us
  transfers between devices with their start and end apart: 36, of which 18 were waited for; matrix products, arithmetic and copies ran while one was open for 17% of the time, Pallas kernels for 0%

profile of v1, /device:TPU:1, one launch (start us, length us, event | category | flops | bytes accessed | tf_op | source)
XLA Modules:
  0.0 367.0 jit_solution(8707376033500493417)
XLA Ops:
  7.3 4.0 %collective-permute-start.1 = (bf16[1,2048,128]{2,1,0:T(8,128)(2,1)}, bf16[1,2048,128]{2,1,0:T(8,128)(2,1)}, u32[]{:S(2)}, u32[]{:S(2)}) collective-permute-start(bf16[1,2048,128]{2,1,0:T(8,128)(2,1)} %param.7), channel_id=1, source_target_pairs={{0,1},{1,2},{2,3},{3,4},{4,5},{5,6},{6,7},{7,8},{8,9},{9,10},{10,1... | collective-permute-start | bytes 1572872 | tf_op jit(solution)/shard_map/ppermute | solution.py:55
  11.3 5.6 %collective-permute-start.2 = (bf16[1,2048,128]{2,1,0:T(8,128)(2,1)}, bf16[1,2048,128]{2,1,0:T(8,128)(2,1)S(1)}, u32[]{:S(2)}, u32[]{:S(2)}) collective-permute-start(bf16[1,2048,128]{2,1,0:T(8,128)(2,1)} %param.7), channel_id=1, source_target_pairs={{0,15},{1,0},{2,1},{3,2},{4,3},{5,4},{6,5},{7,6},{8,7},{9,8},{10,9... | collective-permute-start | bytes 1572872 | tf_op jit(solution)/shard_map/ppermute | solution.py:60
  18.2 8.4 %collective-permute-start.16 = (bf16[1,2048,128]{2,1,0:T(8,128)(2,1)S(1)}, bf16[1,2048,128]{2,1,0:T(8,128)(2,1)}, u32[]{:S(2)}, u32[]{:S(2)}) collective-permute-start(bf16[1,2048,128]{2,1,0:T(8,128)(2,1)S(1)} %convert_element_type.7), channel_id=1, source_target_pairs={{16,0},{32,16},{48,32},{64,48},{80,64},{96,80},{112,96},{128,112},... | collective-permute-start | bytes 1572872 | tf_op jit(solution)/shard_map/ppermute | solution.py:15
  30.5 4.3 %squeeze.86.clone = bf16[2048,2048]{1,0:T(8,128)(2,1)} broadcast(bf16[]{:T(256)} %constant.151.clone.1), dimensions={} | broadcast | bytes 8388610 | tf_op jit(solution)/shard_map/squeeze | solution.py:66
  35.7 4.3 %squeeze.86.clone.1 = bf16[2048,2048]{1,0:T(8,128)(2,1)} broadcast(bf16[]{:T(256)} %constant.151.clone.1), dimensions={} | broadcast | bytes 8388610 | tf_op jit(solution)/shard_map/squeeze | solution.py:66
  40.9 6.7 %collective-permute-start.19 = (bf16[1,2048,128]{2,1,0:T(8,128)(2,1)S(1)}, bf16[1,2048,128]{2,1,0:T(8,128)(2,1)S(1)}, u32[]{:S(2)}, u32[]{:S(2)}) collective-permute-start(bf16[1,2048,128]{2,1,0:T(8,128)(2,1)S(1)} %copy-done.3), channel_id=1, source_target_pairs={{0,15},{1,0},{2,1},{3,2},{4,3},{5,4},{6,5},{7,6},{8,7},{9,8},{10,9... | collective-permute-start | bytes 1572872 | tf_op jit(solution)/shard_map/ppermute | solution.py:60
  47.6 2.0 bitcast_dynamic-update-slice_fusion.30
  52.4 6.6 %collective-permute-start.4 = (bf16[1,2048,128]{2,1,0:T(8,128)(2,1)S(1)}, bf16[1,2048,128]{2,1,0:T(8,128)(2,1)S(1)}, u32[]{:S(2)}, u32[]{:S(2)}) collective-permute-start(bf16[1,2048,128]{2,1,0:T(8,128)(2,1)S(1)} %collective-permute-done.2), channel_id=1, source_target_pairs={{0,15},{1,0},{2,1},{3,2},{4,3},{5,4},{6,5},{7,6},{8,7},{9,8},{10,9... | collective-permute-start | bytes 1572872 | tf_op jit(solution)/shard_map/ppermute | solution.py:60
  63.7 3.6 collective-permute-done.3
  67.3 3.8 %collective-permute-start.21 = (bf16[1,2048,128]{2,1,0:T(8,128)(2,1)S(1)}, bf16[1,2048,128]{2,1,0:T(8,128)(2,1)S(1)}, u32[]{:S(2)}, u32[]{:S(2)}) collective-permute-start(bf16[1,2048,128]{2,1,0:T(8,128)(2,1)S(1)} %collective-permute-done.19), channel_id=1, source_target_pairs={{0,15},{1,0},{2,1},{3,2},{4,3},{5,4},{6,5},{7,6},{8,7},{9,8},{10,9... | collective-permute-start | bytes 1572872 | tf_op jit(solution)/shard_map/ppermute | solution.py:60
  75.0 3.7 %collective-permute-done.20 = bf16[1,2048,128]{2,1,0:T(8,128)(2,1)S(1)} collective-permute-done((bf16[1,2048,128]{2,1,0:T(8,128)(2,1)S(1)}, bf16[1,2048,128]{2,1,0:T(8,128)(2,1)S(1)}, u32[]{:S(2)}, u32[]{:S(2)}) %collective-permute-start.20) | collective-permute-done | bytes 524320 | tf_op jit(solution)/shard_map/ppermute | solution.py:55
  78.7 3.7 %collective-permute-start.6 = (bf16[1,2048,128]{2,1,0:T(8,128)(2,1)S(1)}, bf16[1,2048,128]{2,1,0:T(8,128)(2,1)S(1)}, u32[]{:S(2)}, u32[]{:S(2)}) collective-permute-start(bf16[1,2048,128]{2,1,0:T(8,128)(2,1)S(1)} %collective-permute-done.4), channel_id=1, source_target_pairs={{0,15},{1,0},{2,1},{3,2},{4,3},{5,4},{6,5},{7,6},{8,7},{9,8},{10,9... | collective-permute-start | bytes 1572872 | tf_op jit(solution)/shard_map/ppermute | solution.py:60
  86.1 3.8 %collective-permute-done.5 = bf16[1,2048,128]{2,1,0:T(8,128)(2,1)S(1)} collective-permute-done((bf16[1,2048,128]{2,1,0:T(8,128)(2,1)S(1)}, bf16[1,2048,128]{2,1,0:T(8,128)(2,1)S(1)}, u32[]{:S(2)}, u32[]{:S(2)}) %collective-permute-start.5) | collective-permute-done | bytes 524320 | tf_op jit(solution)/shard_map/ppermute | solution.py:55
  89.9 3.2 collective-permute-start.23
  94.1 2.0 collective-permute-start.7
  97.0 3.7 %collective-permute-done.22 = bf16[1,2048,128]{2,1,0:T(8,128)(2,1)S(1)} collective-permute-done((bf16[1,2048,128]{2,1,0:T(8,128)(2,1)S(1)}, bf16[1,2048,128]{2,1,0:T(8,128)(2,1)S(1)}, u32[]{:S(2)}, u32[]{:S(2)}) %collective-permute-start.22) | collective-permute-done | bytes 524320 | tf_op jit(solution)/shard_map/ppermute | solution.py:55
  100.7 3.4 collective-permute-start.8
  107.8 3.8 %collective-permute-done.7 = bf16[1,2048,128]{2,1,0:T(8,128)(2,1)S(1)} collective-permute-done((bf16[1,2048,128]{2,1,0:T(8,128)(2,1)S(1)}, bf16[1,2048,128]{2,1,0:T(8,128)(2,1)S(1)}, u32[]{:S(2)}, u32[]{:S(2)}) %collective-permute-start.7) | collective-permute-done | bytes 524320 | tf_op jit(solution)/shard_map/ppermute | solution.py:55
  111.6 3.3 collective-permute-start.25
  115.8 2.0 collective-permute-start.9
  118.7 3.7 %collective-permute-done.24 = bf16[1,2048,128]{2,1,0:T(8,128)(2,1)S(1)} collective-permute-done((bf16[1,2048,128]{2,1,0:T(8,128)(2,1)S(1)}, bf16[1,2048,128]{2,1,0:T(8,128)(2,1)S(1)}, u32[]{:S(2)}, u32[]{:S(2)}) %collective-permute-start.24) | collective-permute-done | bytes 524320 | tf_op jit(solution)/shard_map/ppermute | solution.py:55
  122.4 3.4 collective-permute-start.10
  129.6 3.8 %collective-permute-done.9 = bf16[1,2048,128]{2,1,0:T(8,128)(2,1)S(1)} collective-permute-done((bf16[1,2048,128]{2,1,0:T(8,128)(2,1)S(1)}, bf16[1,2048,128]{2,1,0:T(8,128)(2,1)S(1)}, u32[]{:S(2)}, u32[]{:S(2)}) %collective-permute-start.9) | collective-permute-done | bytes 524320 | tf_op jit(solution)/shard_map/ppermute | solution.py:55
  133.4 3.3 collective-permute-start.27
  137.6 2.0 collective-permute-start.11
  140.5 3.8 %collective-permute-done.26 = bf16[1,2048,128]{2,1,0:T(8,128)(2,1)S(1)} collective-permute-done((bf16[1,2048,128]{2,1,0:T(8,128)(2,1)S(1)}, bf16[1,2048,128]{2,1,0:T(8,128)(2,1)S(1)}, u32[]{:S(2)}, u32[]{:S(2)}) %collective-permute-start.26) | collective-permute-done | bytes 524320 | tf_op jit(solution)/shard_map/ppermute | solution.py:55
  144.2 3.4 collective-permute-start.12
  151.4 3.7 %collective-permute-done.11 = bf16[1,2048,128]{2,1,0:T(8,128)(2,1)S(1)} collective-permute-done((bf16[1,2048,128]{2,1,0:T(8,128)(2,1)S(1)}, bf16[1,2048,128]{2,1,0:T(8,128)(2,1)S(1)}, u32[]{:S(2)}, u32[]{:S(2)}) %collective-permute-start.11) | collective-permute-done | bytes 524320 | tf_op jit(solution)/shard_map/ppermute | solution.py:55
  155.1 3.3 collective-permute-start.29
  162.2 3.8 %collective-permute-done.28 = bf16[1,2048,128]{2,1,0:T(8,128)(2,1)S(1)} collective-permute-done((bf16[1,2048,128]{2,1,0:T(8,128)(2,1)S(1)}, bf16[1,2048,128]{2,1,0:T(8,128)(2,1)S(1)}, u32[]{:S(2)}, u32[]{:S(2)}) %collective-permute-start.28) | collective-permute-done | bytes 524320 | tf_op jit(solution)/shard_map/ppermute | solution.py:55
  166.0 3.4 collective-permute-start.14
  170.3 2.1 collective-permute-start.30
  172.4 2.0 bitcast_dynamic-update-slice_fusion.3
  174.3 2.5 collective-permute-done.13
  176.9 4.5 %collective-permute-start.31 = (bf16[1,2048,128]{2,1,0:T(8,128)(2,1)}, bf16[1,2048,128]{2,1,0:T(8,128)(2,1)}, u32[]{:S(2)}, u32[]{:S(2)}) collective-permute-start(bf16[1,2048,128]{2,1,0:T(8,128)(2,1)} %collective-permute-done.29), channel_id=1, source_target_pairs={{0,15},{1,0},{2,1},{3,2},{4,3},{5,4},{6,5},{7,6},{8,7},{9,8},{10,9... | collective-permute-start | bytes 1572872 | tf_op jit(solution)/shard_map/ppermute | solution.py:60
  182.3 5.5 %collective-permute-done.30 = bf16[1,2048,128]{2,1,0:T(8,128)(2,1)} collective-permute-done((bf16[1,2048,128]{2,1,0:T(8,128)(2,1)S(1)}, bf16[1,2048,128]{2,1,0:T(8,128)(2,1)}, u32[]{:S(2)}, u32[]{:S(2)}) %collective-permute-start.30) | collective-permute-done | bytes 524320 | tf_op jit(solution)/shard_map/ppermute | solution.py:55
  189.7 2.0 bitcast_dynamic-update-slice_fusion.2
  191.6 2.1 collective-permute-start.32
  194.6 6.4 %collective-permute-done.15 = bf16[1,2048,128]{2,1,0:T(8,128)(2,1)S(1)} collective-permute-done((bf16[1,2048,128]{2,1,0:T(8,128)(2,1)S(1)}, bf16[1,2048,128]{2,1,0:T(8,128)(2,1)S(1)}, u32[]{:S(2)}, u32[]{:S(2)}) %collective-permute-start.15) | collective-permute-done | bytes 524320 | tf_op jit(solution)/shard_map/ppermute | solution.py:55
  201.9 5.8 %fusion.22 = f32[2048,128]{1,0:T(8,128)S(1)} fusion(bf16[2048,2048]{1,0:T(8,128)(2,1)} %bitcast_dynamic-update-slice_fusion.16, bf16[1,2048,128]{2,1,0:T(8,128)(2,1)} %collective-permute-done.16), kind=kOutput, calls=%fused_computation.26 | convolution fusion | flops 1073741824 | bytes 9961472 | tf_op jit(solution)/shard_map/dot_general | solution.py:66
  208.5 47.7 %all-gather.3.cloned.1.call-done = bf16[1,2048,2048]{2,1,0:T(8,128)(2,1)} async-done(((bf16[1,2048,128]{2,1,0:T(8,128)(2,1)}), bf16[1,2048,2048]{2,1,0:T(8,128)(2,1)}) %all-gather.3.cloned.1.call-update) | async-done | bytes 8388624 | tf_op jit(solution)/shard_map/all_gather | solution.py:40
  256.2 6.6 %fusion.25 = (bf16[2048,128]{1,0:T(8,128)(2,1)}, f32[2048,128]{1,0:T(8,128)S(1)}) fusion(f32[2048,128]{1,0:T(8,128)S(1)} %fusion.22, bf16[1,2048,128]{2,1,0:T(8,128)(2,1)} %copy-done.1, bf16[1,2048,2048]{2,1,0:T(8,128)(2,1)} %all-gather.3.cloned.1.call-done, f32[1,2048,128]{2,1,0:T(8,128)S(1)} %copy-done), kind=kOutput, calls=%fused_computation.45 | convolution fusion | flops 1074528256 | bytes 12582912 | tf_op jit(solution)/shard_map/dot_general | solution.py:65
  264.2 2.0 bitcast_dynamic-update-slice_fusion.1
  268.1 4.2 %collective-permute-start.17 = (bf16[2048,128]{1,0:T(8,128)(2,1)}, bf16[2048,128]{1,0:T(8,128)(2,1)S(1)}, u32[]{:S(2)}, u32[]{:S(2)}) collective-permute-start(bf16[2048,128]{1,0:T(8,128)(2,1)} %get-tuple-element.5), channel_id=1, source_target_pairs={{0,32},{16,48},{32,64},{48,80},{64,96},{80,112},{96,128},{112,144}... | collective-permute-start | bytes 1572872 | tf_op jit(solution)/shard_map/ppermute | solution.py:23
  272.3 4.6 %collective-permute-done.33 = bf16[2048,128]{1,0:T(8,128)(2,1)S(1)} collective-permute-done((bf16[2048,128]{1,0:T(8,128)(2,1)}, bf16[2048,128]{1,0:T(8,128)(2,1)S(1)}, u32[]{:S(2)}, u32[]{:S(2)}) %collective-permute-start.33) | collective-permute-done | bytes 524320 | tf_op jit(solution)/shard_map/ppermute | solution.py:23
  276.8 6.2 %fusion.26 = f32[2048,128]{1,0:T(8,128)S(1)} fusion(bf16[2048,2048]{1,0:T(8,128)(2,1)} %bitcast_dynamic-update-slice_fusion, bf16[2048,128]{1,0:T(8,128)(2,1)S(1)} %collective-permute-done.33), kind=kOutput, calls=%fused_computation.46 | convolution fusion | flops 1073741824 | bytes 9961472 | tf_op jit(solution)/shard_map/dot_general | solution.py:66
  283.0 70.4 %all-gather.5.cloned.1.call-done = bf16[1,2048,2048]{2,1,0:T(8,128)(2,1)} async-done(((bf16[1,2048,128]{2,1,0:T(8,128)(2,1)}), bf16[1,2048,2048]{2,1,0:T(8,128)(2,1)}) %all-gather.5.cloned.1.call-update) | async-done | bytes 8388624 | tf_op jit(solution)/shard_map/all_gather | solution.py:40
  353.5 6.7 %fusion.19 = f32[1,2048,128]{2,1,0:T(8,128)} fusion(f32[2048,128]{1,0:T(8,128)S(1)} %get-tuple-element.6, f32[2048,128]{1,0:T(8,128)S(1)} %fusion.26, bf16[2048,128]{1,0:T(8,128)(2,1)S(1)} %collective-permute-done.17, bf16[1,2048,2048]{2,1,0:T(8,128)(2,1)} %all-gather.5.cloned.1.call-done), kind=kOutput, calls=%fused_computation.9 | convolution fusion | flops 1074266112 | bytes 12058624 | tf_op jit(solution)/shard_map/dot_general | solution.py:65
  (73 shorter events, 52.6 us)
Async XLA Ops:
  6.5 28.3 %copy-start.2 = (bf16[1,2048,128]{2,1,0:T(8,128)(2,1)S(1)}, bf16[1,2048,128]{2,1,0:T(8,128)(2,1)}, u32[]{:S(2)}) copy-start(bf16[1,2048,128]{2,1,0:T(8,128)(2,1)} %param.7) | copy-start | bytes 1572868
  6.5 249.7 %all-gather.3.cloned.1.call-start = ((), (), s32[]{:S(2)}) async-start(), calls=%async_computation | async-start | bytes 8912896 | tf_op jit(solution)/shard_map/all_gather | solution.py:40
  7.3 346.2 %all-gather.5.cloned.1.call-start = ((), (), s32[]{:S(2)}) async-start(), calls=%async_computation.1 | async-start | bytes 8912896 | tf_op jit(solution)/shard_map/all_gather | solution.py:40
  7.3 33.6 %collective-permute-start.1 = (bf16[1,2048,128]{2,1,0:T(8,128)(2,1)}, bf16[1,2048,128]{2,1,0:T(8,128)(2,1)}, u32[]{:S(2)}, u32[]{:S(2)}) collective-permute-start(bf16[1,2048,128]{2,1,0:T(8,128)(2,1)} %param.7), channel_id=1, source_target_pairs={{0,1},{1,2},{2,3},{3,4},{4,5},{5,6},{6,7},{7,8},{8,9},{9,10},{10,1... | collective-permute-start | bytes 1572872 | tf_op jit(solution)/shard_map/ppermute | solution.py:55
  11.3 38.3 %collective-permute-start.2 = (bf16[1,2048,128]{2,1,0:T(8,128)(2,1)}, bf16[1,2048,128]{2,1,0:T(8,128)(2,1)S(1)}, u32[]{:S(2)}, u32[]{:S(2)}) collective-permute-start(bf16[1,2048,128]{2,1,0:T(8,128)(2,1)} %param.7), channel_id=1, source_target_pairs={{0,15},{1,0},{2,1},{3,2},{4,3},{5,4},{6,5},{7,6},{8,7},{9,8},{10,9... | collective-permute-start | bytes 1572872 | tf_op jit(solution)/shard_map/ppermute | solution.py:60
  18.2 183.7 %collective-permute-start.16 = (bf16[1,2048,128]{2,1,0:T(8,128)(2,1)S(1)}, bf16[1,2048,128]{2,1,0:T(8,128)(2,1)}, u32[]{:S(2)}, u32[]{:S(2)}) collective-permute-start(bf16[1,2048,128]{2,1,0:T(8,128)(2,1)S(1)} %convert_element_type.7), channel_id=1, source_target_pairs={{16,0},{32,16},{48,32},{64,48},{80,64},{96,80},{112,96},{128,112},... | collective-permute-start | bytes 1572872 | tf_op jit(solution)/shard_map/ppermute | solution.py:15
  26.6 181.2 %collective-permute-start = (bf16[1,2048,128]{2,1,0:T(8,128)(2,1)S(1)}, bf16[1,2048,128]{2,1,0:T(8,128)(2,1)S(1)}, u32[]{:S(2)}, u32[]{:S(2)}) collective-permute-start(bf16[1,2048,128]{2,1,0:T(8,128)(2,1)S(1)} %convert_element_type.7), channel_id=1, source_target_pairs={{0,16},{16,32},{32,48},{48,64},{64,80},{80,96},{96,112},{112,128},... | collective-permute-start | bytes 1572872 | tf_op jit(solution)/shard_map/ppermute | solution.py:14
  28.5 23.9 %collective-permute-start.18 = (bf16[1,2048,128]{2,1,0:T(8,128)(2,1)}, bf16[1,2048,128]{2,1,0:T(8,128)(2,1)S(1)}, u32[]{:S(2)}, u32[]{:S(2)}) collective-permute-start(bf16[1,2048,128]{2,1,0:T(8,128)(2,1)} %param.9), channel_id=1, source_target_pairs={{0,1},{1,2},{2,3},{3,4},{4,5},{5,6},{6,7},{7,8},{8,9},{9,10},{10,1... | collective-permute-start | bytes 1572872 | tf_op jit(solution)/shard_map/ppermute | solution.py:55
  30.4 9.5 %copy-start.3 = (bf16[1,2048,128]{2,1,0:T(8,128)(2,1)S(1)}, bf16[1,2048,128]{2,1,0:T(8,128)(2,1)}, u32[]{:S(2)}) copy-start(bf16[1,2048,128]{2,1,0:T(8,128)(2,1)} %param.9) | copy-start | bytes 1572868
  40.9 20.0 %collective-permute-start.19 = (bf16[1,2048,128]{2,1,0:T(8,128)(2,1)S(1)}, bf16[1,2048,128]{2,1,0:T(8,128)(2,1)S(1)}, u32[]{:S(2)}, u32[]{:S(2)}) collective-permute-start(bf16[1,2048,128]{2,1,0:T(8,128)(2,1)S(1)} %copy-done.3), channel_id=1, source_target_pairs={{0,15},{1,0},{2,1},{3,2},{4,3},{5,4},{6,5},{7,6},{8,7},{9,8},{10,9... | collective-permute-start | bytes 1572872 | tf_op jit(solution)/shard_map/ppermute | solution.py:60
  49.6 17.7 %collective-permute-start.3 = (bf16[1,2048,128]{2,1,0:T(8,128)(2,1)}, bf16[1,2048,128]{2,1,0:T(8,128)(2,1)S(1)}, u32[]{:S(2)}, u32[]{:S(2)}) collective-permute-start(bf16[1,2048,128]{2,1,0:T(8,128)(2,1)} %collective-permute-done.1), channel_id=1, source_target_pairs={{0,1},{1,2},{2,3},{3,4},{4,5},{5,6},{6,7},{7,8},{8,9},{9,10},{10,1... | collective-permute-start | bytes 1572872 | tf_op jit(solution)/shard_map/ppermute | solution.py:55
  52.4 19.7 %collective-permute-start.4 = (bf16[1,2048,128]{2,1,0:T(8,128)(2,1)S(1)}, bf16[1,2048,128]{2,1,0:T(8,128)(2,1)S(1)}, u32[]{:S(2)}, u32[]{:S(2)}) collective-permute-start(bf16[1,2048,128]{2,1,0:T(8,128)(2,1)S(1)} %collective-permute-done.2), channel_id=1, source_target_pairs={{0,15},{1,0},{2,1},{3,2},{4,3},{5,4},{6,5},{7,6},{8,7},{9,8},{10,9... | collective-permute-start | bytes 1572872 | tf_op jit(solution)/shard_map/ppermute | solution.py:60
  60.9 17.8 %collective-permute-start.20 = (bf16[1,2048,128]{2,1,0:T(8,128)(2,1)S(1)}, bf16[1,2048,128]{2,1,0:T(8,128)(2,1)S(1)}, u32[]{:S(2)}, u32[]{:S(2)}) collective-permute-start(bf16[1,2048,128]{2,1,0:T(8,128)(2,1)S(1)} %collective-permute-done.18), channel_id=1, source_target_pairs={{0,1},{1,2},{2,3},{3,4},{4,5},{5,6},{6,7},{7,8},{8,9},{9,10},{10,1... | collective-permute-start | bytes 1572872 | tf_op jit(solution)/shard_map/ppermute | solution.py:55
  67.3 15.9 %collective-permute-start.21 = (bf16[1,2048,128]{2,1,0:T(8,128)(2,1)S(1)}, bf16[1,2048,128]{2,1,0:T(8,128)(2,1)S(1)}, u32[]{:S(2)}, u32[]{:S(2)}) collective-permute-start(bf16[1,2048,128]{2,1,0:T(8,128)(2,1)S(1)} %collective-permute-done.19), channel_id=1, source_target_pairs={{0,15},{1,0},{2,1},{3,2},{4,3},{5,4},{6,5},{7,6},{8,7},{9,8},{10,9... | collective-permute-start | bytes 1572872 | tf_op jit(solution)/shard_map/ppermute | solution.py:60
  72.1 17.8 %collective-permute-start.5 = (bf16[1,2048,128]{2,1,0:T(8,128)(2,1)S(1)}, bf16[1,2048,128]{2,1,0:T(8,128)(2,1)S(1)}, u32[]{:S(2)}, u32[]{:S(2)}) collective-permute-start(bf16[1,2048,128]{2,1,0:T(8,128)(2,1)S(1)} %collective-permute-done.3), channel_id=1, source_target_pairs={{0,1},{1,2},{2,3},{3,4},{4,5},{5,6},{6,7},{7,8},{8,9},{9,10},{10,1... | collective-permute-start | bytes 1572872 | tf_op jit(solution)/shard_map/ppermute | solution.py:55
  78.7 15.4 %collective-permute-start.6 = (bf16[1,2048,128]{2,1,0:T(8,128)(2,1)S(1)}, bf16[1,2048,128]{2,1,0:T(8,128)(2,1)S(1)}, u32[]{:S(2)}, u32[]{:S(2)}) collective-permute-start(bf16[1,2048,128]{2,1,0:T(8,128)(2,1)S(1)} %collective-permute-done.4), channel_id=1, source_target_pairs={{0,15},{1,0},{2,1},{3,2},{4,3},{5,4},{6,5},{7,6},{8,7},{9,8},{10,9... | collective-permute-start | bytes 1572872 | tf_op jit(solution)/shard_map/ppermute | solution.py:60
  83.2 17.4 %collective-permute-start.22 = (bf16[1,2048,128]{2,1,0:T(8,128)(2,1)S(1)}, bf16[1,2048,128]{2,1,0:T(8,128)(2,1)S(1)}, u32[]{:S(2)}, u32[]{:S(2)}) collective-permute-start(bf16[1,2048,128]{2,1,0:T(8,128)(2,1)S(1)} %collective-permute-done.20), channel_id=1, source_target_pairs={{0,1},{1,2},{2,3},{3,4},{4,5},{5,6},{6,7},{7,8},{8,9},{9,10},{10,1... | collective-permute-start | bytes 1572872 | tf_op jit(solution)/shard_map/ppermute | solution.py:55
  89.9 15.1 %collective-permute-start.23 = (bf16[1,2048,128]{2,1,0:T(8,128)(2,1)S(1)}, bf16[1,2048,128]{2,1,0:T(8,128)(2,1)S(1)}, u32[]{:S(2)}, u32[]{:S(2)}) collective-permute-start(bf16[1,2048,128]{2,1,0:T(8,128)(2,1)S(1)} %collective-permute-done.21), channel_id=1, source_target_pairs={{0,15},{1,0},{2,1},{3,2},{4,3},{5,4},{6,5},{7,6},{8,7},{9,8},{10,9... | collective-permute-start | bytes 1572872 | tf_op jit(solution)/shard_map/ppermute | solution.py:60
  94.1 17.5 %collective-permute-start.7 = (bf16[1,2048,128]{2,1,0:T(8,128)(2,1)S(1)}, bf16[1,2048,128]{2,1,0:T(8,128)(2,1)S(1)}, u32[]{:S(2)}, u32[]{:S(2)}) collective-permute-start(bf16[1,2048,128]{2,1,0:T(8,128)(2,1)S(1)} %collective-permute-done.5), channel_id=1, source_target_pairs={{0,1},{1,2},{2,3},{3,4},{4,5},{5,6},{6,7},{7,8},{8,9},{9,10},{10,1... | collective-permute-start | bytes 1572872 | tf_op jit(solution)/shard_map/ppermute | solution.py:55
  100.7 15.1 %collective-permute-start.8 = (bf16[1,2048,128]{2,1,0:T(8,128)(2,1)S(1)}, bf16[1,2048,128]{2,1,0:T(8,128)(2,1)S(1)}, u32[]{:S(2)}, u32[]{:S(2)}) collective-permute-start(bf16[1,2048,128]{2,1,0:T(8,128)(2,1)S(1)} %collective-permute-done.6), channel_id=1, source_target_pairs={{0,15},{1,0},{2,1},{3,2},{4,3},{5,4},{6,5},{7,6},{8,7},{9,8},{10,9... | collective-permute-start | bytes 1572872 | tf_op jit(solution)/shard_map/ppermute | solution.py:60
  105.0 17.5 %collective-permute-start.24 = (bf16[1,2048,128]{2,1,0:T(8,128)(2,1)S(1)}, bf16[1,2048,128]{2,1,0:T(8,128)(2,1)S(1)}, u32[]{:S(2)}, u32[]{:S(2)}) collective-permute-start(bf16[1,2048,128]{2,1,0:T(8,128)(2,1)S(1)} %collective-permute-done.22), channel_id=1, source_target_pairs={{0,1},{1,2},{2,3},{3,4},{4,5},{5,6},{6,7},{7,8},{8,9},{9,10},{10,1... | collective-permute-start | bytes 1572872 | tf_op jit(solution)/shard_map/ppermute | solution.py:55
  111.6 15.2 %collective-permute-start.25 = (bf16[1,2048,128]{2,1,0:T(8,128)(2,1)S(1)}, bf16[1,2048,128]{2,1,0:T(8,128)(2,1)S(1)}, u32[]{:S(2)}, u32[]{:S(2)}) collective-permute-start(bf16[1,2048,128]{2,1,0:T(8,128)(2,1)S(1)} %collective-permute-done.23), channel_id=1, source_target_pairs={{0,15},{1,0},{2,1},{3,2},{4,3},{5,4},{6,5},{7,6},{8,7},{9,8},{10,9... | collective-permute-start | bytes 1572872 | tf_op jit(solution)/shard_map/ppermute | solution.py:60
  115.8 17.6 %collective-permute-start.9 = (bf16[1,2048,128]{2,1,0:T(8,128)(2,1)S(1)}, bf16[1,2048,128]{2,1,0:T(8,128)(2,1)S(1)}, u32[]{:S(2)}, u32[]{:S(2)}) collective-permute-start(bf16[1,2048,128]{2,1,0:T(8,128)(2,1)S(1)} %collective-permute-done.7), channel_id=1, source_target_pairs={{0,1},{1,2},{2,3},{3,4},{4,5},{5,6},{6,7},{7,8},{8,9},{9,10},{10,1... | collective-permute-start | bytes 1572872 | tf_op jit(solution)/shard_map/ppermute | solution.py:55
  122.4 15.1 %collective-permute-start.10 = (bf16[1,2048,128]{2,1,0:T(8,128)(2,1)S(1)}, bf16[1,2048,128]{2,1,0:T(8,128)(2,1)S(1)}, u32[]{:S(2)}, u32[]{:S(2)}) collective-permute-start(bf16[1,2048,128]{2,1,0:T(8,128)(2,1)S(1)} %collective-permute-done.8), channel_id=1, source_target_pairs={{0,15},{1,0},{2,1},{3,2},{4,3},{5,4},{6,5},{7,6},{8,7},{9,8},{10,9... | collective-permute-start | bytes 1572872 | tf_op jit(solution)/shard_map/ppermute | solution.py:60
  126.8 17.4 %collective-permute-start.26 = (bf16[1,2048,128]{2,1,0:T(8,128)(2,1)S(1)}, bf16[1,2048,128]{2,1,0:T(8,128)(2,1)S(1)}, u32[]{:S(2)}, u32[]{:S(2)}) collective-permute-start(bf16[1,2048,128]{2,1,0:T(8,128)(2,1)S(1)} %collective-permute-done.24), channel_id=1, source_target_pairs={{0,1},{1,2},{2,3},{3,4},{4,5},{5,6},{6,7},{7,8},{8,9},{9,10},{10,1... | collective-permute-start | bytes 1572872 | tf_op jit(solution)/shard_map/ppermute | solution.py:55
  133.4 15.2 %collective-permute-start.27 = (bf16[1,2048,128]{2,1,0:T(8,128)(2,1)S(1)}, bf16[1,2048,128]{2,1,0:T(8,128)(2,1)S(1)}, u32[]{:S(2)}, u32[]{:S(2)}) collective-permute-start(bf16[1,2048,128]{2,1,0:T(8,128)(2,1)S(1)} %collective-permute-done.25), channel_id=1, source_target_pairs={{0,15},{1,0},{2,1},{3,2},{4,3},{5,4},{6,5},{7,6},{8,7},{9,8},{10,9... | collective-permute-start | bytes 1572872 | tf_op jit(solution)/shard_map/ppermute | solution.py:60
  137.6 17.6 %collective-permute-start.11 = (bf16[1,2048,128]{2,1,0:T(8,128)(2,1)S(1)}, bf16[1,2048,128]{2,1,0:T(8,128)(2,1)S(1)}, u32[]{:S(2)}, u32[]{:S(2)}) collective-permute-start(bf16[1,2048,128]{2,1,0:T(8,128)(2,1)S(1)} %collective-permute-done.9), channel_id=1, source_target_pairs={{0,1},{1,2},{2,3},{3,4},{4,5},{5,6},{6,7},{7,8},{8,9},{9,10},{10,1... | collective-permute-start | bytes 1572872 | tf_op jit(solution)/shard_map/ppermute | solution.py:55
  144.2 15.1 %collective-permute-start.12 = (bf16[1,2048,128]{2,1,0:T(8,128)(2,1)S(1)}, bf16[1,2048,128]{2,1,0:T(8,128)(2,1)S(1)}, u32[]{:S(2)}, u32[]{:S(2)}) collective-permute-start(bf16[1,2048,128]{2,1,0:T(8,128)(2,1)S(1)} %collective-permute-done.10), channel_id=1, source_target_pairs={{0,15},{1,0},{2,1},{3,2},{4,3},{5,4},{6,5},{7,6},{8,7},{9,8},{10,9... | collective-permute-start | bytes 1572872 | tf_op jit(solution)/shard_map/ppermute | solution.py:60
  148.6 17.4 %collective-permute-start.28 = (bf16[1,2048,128]{2,1,0:T(8,128)(2,1)S(1)}, bf16[1,2048,128]{2,1,0:T(8,128)(2,1)S(1)}, u32[]{:S(2)}, u32[]{:S(2)}) collective-permute-start(bf16[1,2048,128]{2,1,0:T(8,128)(2,1)S(1)} %collective-permute-done.26), channel_id=1, source_target_pairs={{0,1},{1,2},{2,3},{3,4},{4,5},{5,6},{6,7},{7,8},{8,9},{9,10},{10,1... | collective-permute-start | bytes 1572872 | tf_op jit(solution)/shard_map/ppermute | solution.py:55
  155.1 15.1 %collective-permute-start.29 = (bf16[1,2048,128]{2,1,0:T(8,128)(2,1)S(1)}, bf16[1,2048,128]{2,1,0:T(8,128)(2,1)}, u32[]{:S(2)}, u32[]{:S(2)}) collective-permute-start(bf16[1,2048,128]{2,1,0:T(8,128)(2,1)S(1)} %collective-permute-done.27), channel_id=1, source_target_pairs={{0,15},{1,0},{2,1},{3,2},{4,3},{5,4},{6,5},{7,6},{8,7},{9,8},{10,9... | collective-permute-start | bytes 1572872 | tf_op jit(solution)/shard_map/ppermute | solution.py:60
  159.3 17.6 %collective-permute-start.13 = (bf16[1,2048,128]{2,1,0:T(8,128)(2,1)S(1)}, bf16[1,2048,128]{2,1,0:T(8,128)(2,1)S(1)}, u32[]{:S(2)}, u32[]{:S(2)}) collective-permute-start(bf16[1,2048,128]{2,1,0:T(8,128)(2,1)S(1)} %collective-permute-done.11), channel_id=1, source_target_pairs={{0,1},{1,2},{2,3},{3,4},{4,5},{5,6},{6,7},{7,8},{8,9},{9,10},{10,1... | collective-permute-start | bytes 1572872 | tf_op jit(solution)/shard_map/ppermute | solution.py:55
  166.0 25.7 %collective-permute-start.14 = (bf16[1,2048,128]{2,1,0:T(8,128)(2,1)S(1)}, bf16[1,2048,128]{2,1,0:T(8,128)(2,1)S(1)}, u32[]{:S(2)}, u32[]{:S(2)}) collective-permute-start(bf16[1,2048,128]{2,1,0:T(8,128)(2,1)S(1)} %collective-permute-done.12), channel_id=1, source_target_pairs={{0,15},{1,0},{2,1},{3,2},{4,3},{5,4},{6,5},{7,6},{8,7},{9,8},{10,9... | collective-permute-start | bytes 1572872 | tf_op jit(solution)/shard_map/ppermute | solution.py:60
  170.3 86.0 %copy-start = (f32[1,2048,128]{2,1,0:T(8,128)S(1)}, f32[1,2048,128]{2,1,0:T(8,128)}, u32[]{:S(2)}) copy-start(f32[1,2048,128]{2,1,0:T(8,128)} %param.5) | copy-start | bytes 3145732
  170.3 17.5 %collective-permute-start.30 = (bf16[1,2048,128]{2,1,0:T(8,128)(2,1)S(1)}, bf16[1,2048,128]{2,1,0:T(8,128)(2,1)}, u32[]{:S(2)}, u32[]{:S(2)}) collective-permute-start(bf16[1,2048,128]{2,1,0:T(8,128)(2,1)S(1)} %collective-permute-done.28), channel_id=1, source_target_pairs={{0,1},{1,2},{2,3},{3,4},{4,5},{5,6},{6,7},{7,8},{8,9},{9,10},{10,1... | collective-permute-start | bytes 1572872 | tf_op jit(solution)/shard_map/ppermute | solution.py:55
  176.9 87.3 %collective-permute-start.31 = (bf16[1,2048,128]{2,1,0:T(8,128)(2,1)}, bf16[1,2048,128]{2,1,0:T(8,128)(2,1)}, u32[]{:S(2)}, u32[]{:S(2)}) collective-permute-start(bf16[1,2048,128]{2,1,0:T(8,128)(2,1)} %collective-permute-done.29), channel_id=1, source_target_pairs={{0,15},{1,0},{2,1},{3,2},{4,3},{5,4},{6,5},{7,6},{8,7},{9,8},{10,9... | collective-permute-start | bytes 1572872 | tf_op jit(solution)/shard_map/ppermute | solution.py:60
  187.7 13.2 %collective-permute-start.15 = (bf16[1,2048,128]{2,1,0:T(8,128)(2,1)S(1)}, bf16[1,2048,128]{2,1,0:T(8,128)(2,1)S(1)}, u32[]{:S(2)}, u32[]{:S(2)}) collective-permute-start(bf16[1,2048,128]{2,1,0:T(8,128)(2,1)S(1)} %collective-permute-done.13), channel_id=1, source_target_pairs={{0,1},{1,2},{2,3},{3,4},{4,5},{5,6},{6,7},{7,8},{8,9},{9,10},{10,1... | collective-permute-start | bytes 1572872 | tf_op jit(solution)/shard_map/ppermute | solution.py:55
  191.6 74.5 %collective-permute-start.32 = (bf16[1,2048,128]{2,1,0:T(8,128)(2,1)}, bf16[1,2048,128]{2,1,0:T(8,128)(2,1)}, u32[]{:S(2)}, u32[]{:S(2)}) collective-permute-start(bf16[1,2048,128]{2,1,0:T(8,128)(2,1)} %collective-permute-done.30), channel_id=1, source_target_pairs={{0,1},{1,2},{2,3},{3,4},{4,5},{5,6},{6,7},{7,8},{8,9},{9,10},{10,1... | collective-permute-start | bytes 1572872 | tf_op jit(solution)/shard_map/ppermute | solution.py:55
  207.7 0.8 copy-start.1
  262.9 14.0 %collective-permute-start.33 = (bf16[2048,128]{1,0:T(8,128)(2,1)}, bf16[2048,128]{1,0:T(8,128)(2,1)S(1)}, u32[]{:S(2)}, u32[]{:S(2)}) collective-permute-start(bf16[2048,128]{1,0:T(8,128)(2,1)} %get-tuple-element.5), channel_id=1, source_target_pairs={{32,0},{48,16},{64,32},{80,48},{96,64},{112,80},{128,96},{144,112}... | collective-permute-start | bytes 1572872 | tf_op jit(solution)/shard_map/ppermute | solution.py:23
  268.1 85.4 %collective-permute-start.17 = (bf16[2048,128]{1,0:T(8,128)(2,1)}, bf16[2048,128]{1,0:T(8,128)(2,1)S(1)}, u32[]{:S(2)}, u32[]{:S(2)}) collective-permute-start(bf16[2048,128]{1,0:T(8,128)(2,1)} %get-tuple-element.5), channel_id=1, source_target_pairs={{0,32},{16,48},{32,64},{48,80},{64,96},{80,112},{96,128},{112,144}... | collective-permute-start | bytes 1572872 | tf_op jit(solution)/shard_map/ppermute | solution.py:23
Sparse Core Ops, SparseCore 0:
  10.3 245.8 all-gather.2
  259.2 94.1 all-gather.4
